TPU v7x, 512 devices: a whole 4x8x8 slice. The times are simulated.
512 devices in a mesh: freq: 4 (over z_hi), layer: 8 (over x, z_lo), lat: 16 (over y, core).
Axes of the slice: x: 4, y: 8, z: 8 (z_hi: 4, z_lo: 2; z = z_hi * 2 + z_lo), core: 2. Of those that a mesh axis runs over, the one named last changes fastest.
Arguments:
- source: float32 [2, 4, 2, 8, 512, 512], P(None, 'freq', None, 'layer', 'lat'), may hold values from -6 to 6
- contrast: float32 [2, 4, 8, 512, 512], P(None, 'freq', 'layer', 'lat'), may hold values from -0.5 to 0.5
- green: float32 [2, 4, 8, 8, 512, 512], P(None, 'freq', None, 'layer', 'lat'), may hold values from -0.6 to 0.6
- efield: float32 [2, 4, 2, 8, 512, 512], P(None, 'freq', None, 'layer', 'lat'), may hold values from -6 to 6
- cell_class: int32 [8, 512, 512], P('layer', 'lat'), may hold values from 0 to 7
Outputs:
- cell_gradient: float32 [8, 512, 512], P('layer', 'lat')
- class_gradient: float32 [8, 8], P('layer')
All inputs are finite; a program needn't handle non-finite values.
Results may differ from a plain program's by a relative error of at most 0.0001.
Values sent between devices are 32-bit elements; how exact they have to be, the bound alone decides.
A program may use at most 64 MiB of HBM per device.

v0:
```python
import math

import jax
import jax.numpy as jnp
from jax import lax
from jax.sharding import PartitionSpec as P

NXY = 512
ITERS = 2
CLASSES = 8


highest = lax.Precision.HIGHEST


def tables(length):
    index = jnp.arange(length, dtype=jnp.int32)
    phase = index[:, None] * index[None, :] % length
    angle = phase.astype(jnp.float32) * (2.0 * math.pi / length)
    factor = 1.0 / math.sqrt(length)
    return (jnp.cos(angle) * factor, jnp.sin(angle) * factor)


def forward(field, cosine, sine):
    first = jnp.einsum("zfplxy,yk->zfplkx", field, cosine, precision=highest)
    second = jnp.einsum("zfplxy,yk->zfplkx", field, sine, precision=highest)
    partial_spec = jnp.stack([first[0] + second[1], first[1] - second[0]])
    turned = lax.all_to_all(partial_spec, "lat", split_axis=4, concat_axis=5, tiled=True)
    first = jnp.einsum("zfplkx,xq->zfplkq", turned, cosine, precision=highest)
    second = jnp.einsum("zfplkx,xq->zfplkq", turned, sine, precision=highest)
    return jnp.stack([first[0] + second[1], first[1] - second[0]])


def inverse(mixed, cosine, sine):
    first = jnp.einsum("lzfpkq,qx->zfplkx", mixed, cosine, precision=highest)
    second = jnp.einsum("lzfpkq,qx->zfplkx", mixed, sine, precision=highest)
    half_back = jnp.stack([first[0] - second[1], first[1] + second[0]])
    turned = lax.all_to_all(half_back, "lat", split_axis=5, concat_axis=4, tiled=True)
    first = jnp.einsum("zfplkx,ky->zfplxy", turned, cosine, precision=highest)
    second = jnp.einsum("zfplkx,ky->zfplxy", turned, sine, precision=highest)
    return jnp.stack([first[0] - second[1], first[1] + second[0]])


def couple_product(left, right):
    return jnp.einsum("foiyx,fpiyx->ofpyx", left, right, precision=highest)


def couple(kernel, spectra):
    real_part = couple_product(kernel[0], spectra[0]) - couple_product(kernel[1], spectra[1])
    imag_part = couple_product(kernel[0], spectra[1]) + couple_product(kernel[1], spectra[0])
    return jnp.stack([real_part, imag_part], axis=1)


def cmul(factor, field):
    return jnp.stack(
        [factor[0] * field[0] - factor[1] * field[1], factor[0] * field[1] + factor[1] * field[0]]
    )


def per_device(source, contrast, green, efield, cell_class):
    cosine, sine = tables(source.shape[5])
    factor = contrast[:, :, None]
    field = source
    for step in range(ITERS):
        spectra = forward(cmul(factor, field), cosine, sine)
        mixed = lax.psum_scatter(couple(green, spectra), "layer", scatter_dimension=0, tiled=True)
        field = source + cmul(factor, inverse(mixed, cosine, sine))
    cell_terms = jnp.sum(efield[0] * field[0] - efield[1] * field[1], axis=(0, 1))
    cell = lax.psum(cell_terms, "freq")
    onehot = (cell_class[None] == jnp.arange(CLASSES, dtype=jnp.int32)[:, None, None, None]).astype(
        jnp.float32
    )
    local_sums = jnp.einsum("clxy,lxy->lc", onehot, cell, precision=highest) / float(NXY)
    classes = lax.psum(local_sums, "lat")
    return (cell, classes)


def solution(mesh):
    placed = (
        P(None, "freq", None, "layer", "lat", None),
        P(None, "freq", "layer", "lat", None),
        P(None, "freq", None, "layer", "lat", None),
        P(None, "freq", None, "layer", "lat", None),
        P("layer", "lat", None),
    )
    return jax.shard_map(
        per_device,
        mesh=mesh,
        in_specs=placed,
        out_specs=(P("layer", "lat", None), P("layer", None)),
        check_vma=False,
    )
```

profile of v0, /device:TPU:1, one launch (start us, length us, event | category | flops | bytes accessed | tf_op | source)
XLA Modules:
  0.0 504.2 jit_solution(15579151255789575674)
XLA Ops:
  7.2 0.9 slice_bitcast_fusion.3
  8.0 1.0 multiply_subtract_fusion.3
  9.1 4.9 convolution_bitcast_fusion.6
  14.0 4.9 convolution_bitcast_fusion.7
  19.0 0.7 copy.35
  19.7 1.7 reshape.508
  21.4 10.2 %all-to-all-start = ((f32[16,1,4096]{2,1,0:T(1,128)}), f32[16,1,4096]{2,1,0:T(1,128)S(1)}, u32[]{:S(2)}, u32[]{:S(2)}) async-start(f32[16,1,4096]{2,1,0:T(1,128)} %reshape.508), calls=%async_computation | async-start | bytes 524288 | tf_op jit(solution)/shard_map/all_to_all | solution.py:28
  31.9 11.4 %all-to-all-done = f32[16,1,4096]{2,1,0:T(1,128)S(1)} async-done(((f32[16,1,4096]{2,1,0:T(1,128)}), f32[16,1,4096]{2,1,0:T(1,128)S(1)}, u32[]{:S(2)}, u32[]{:S(2)}) %all-to-all-start) | async-done | bytes 262176 | tf_op jit(solution)/shard_map/all_to_all | solution.py:28
  43.9 1.3 reduce.2
  45.1 0.9 reshape.509
  47.1 4.9 fusion.14
  52.0 4.9 fusion.26
  57.2 1.5 pad_maximum_fusion
  59.0 1.3 dynamic-slice
  60.3 111.5 %all-reduce.8.cloned.1.call-done = f32[8,2,1,2,32,512]{5,4,3,0,2,1:T(8,128)} async-done(((f32[8,2,1,2,32,512]{5,4,3,0,2,1:T(8,128)}), f32[8,2,1,2,32,512]{5,4,3,0,2,1:T(8,128)}) %all-reduce.8.cloned.1.call-update) | async-done | bytes 2097168
  171.8 6.5 %convolution_bitcast_fusion.4 = f32[2,1,2,1,32,512]{5,4,2,0,1,3:T(8,128)S(1)} fusion(f32[8,2,1,2,32,512]{5,4,3,0,2,1:T(8,128)} %all-reduce.8.cloned.1.call-done, u32[]{:T(128)} %bitcast.104), kind=kOutput, calls=%fused_computation.9 | convolution fusion | flops 406585344 | bytes 524800 | tf_op jit(solution)/shard_map/lzfpkq,qx->zfplkx/dot_general | solution.py:36
  178.3 6.5 %convolution_bitcast_fusion.5 = f32[2,1,2,1,32,512]{5,4,2,0,1,3:T(8,128)S(1)} fusion(f32[8,2,1,2,32,512]{5,4,3,0,2,1:T(8,128)} %all-reduce.8.cloned.1.call-done, u32[]{:T(128)} %bitcast.104), kind=kOutput, calls=%fused_computation.10 | convolution fusion | flops 406585344 | bytes 524800 | tf_op jit(solution)/shard_map/lzfpkq,qx->zfplkx/dot_general | solution.py:35
  184.9 0.7 copy.37
  185.6 1.0 reshape.510
  186.7 20.0 %all_to_all.60 = f32[16,1,4096]{2,1,0:T(1,128)S(1)} all-to-all(f32[16,1,4096]{2,1,0:T(1,128)S(1)} %reshape.510), channel_id=1, replica_groups=mesh['freq'=4,'layer'=8,'lat'=16] {'lat'}, dimensions={0} | all-to-all | bytes 524288 | tf_op jit(solution)/shard_map/all_to_all | solution.py:38
  206.7 1.3 reduce.3
  208.0 0.9 reshape.511
  209.9 4.9 fusion.11
  214.8 4.9 fusion.23
  219.9 4.9 convolution_bitcast_fusion.3
  224.8 5.1 %convolution_bitcast_fusion.2 = f32[2,1,2,1,512,32]{4,5,2,0,3,1:T(8,128)S(1)} fusion(f32[1,1,2,1,32,512]{5,4,2,0,3,1:T(8,128)S(1)} %get-tuple-element.25, f32[1,1,2,1,32,512]{5,4,2,0,3,1:T(8,128)S(1)} %get-tuple-element.24), kind=kOutput, calls=%fused_computation.7 | convolution fusion | flops 406650880 | bytes 524288 | tf_op jit(solution)/shard_map/zfplxy,yk->zfplkx/dot_general | solution.py:26
  230.0 0.7 copy.40
  230.7 1.0 reshape.512
  231.8 14.4 %all_to_all.61 = f32[16,1,4096]{2,1,0:T(1,128)S(1)} all-to-all(f32[16,1,4096]{2,1,0:T(1,128)S(1)} %reshape.512), channel_id=1, replica_groups=mesh['freq'=4,'layer'=8,'lat'=16] {'lat'}, dimensions={0} | all-to-all | bytes 524288 | tf_op jit(solution)/shard_map/all_to_all | solution.py:28
  246.2 1.3 reduce.4
  247.4 0.9 reshape.513
  249.4 4.9 fusion.20
  254.3 4.9 fusion.8
  259.6 1.5 pad_maximum_fusion.1
  261.1 109.4 %all-reduce.10.cloned.1.call-done = f32[8,2,1,2,32,512]{5,4,3,0,2,1:T(8,128)} async-done(((f32[8,2,1,2,32,512]{5,4,3,0,2,1:T(8,128)}), f32[8,2,1,2,32,512]{5,4,3,0,2,1:T(8,128)}) %all-reduce.10.cloned.1.call-update) | async-done | bytes 2097168
  370.6 6.7 %convolution_bitcast_fusion.1 = f32[2,1,2,1,32,512]{5,4,2,0,1,3:T(8,128)S(1)} fusion(f32[8,2,1,2,32,512]{5,4,3,0,2,1:T(8,128)} %all-reduce.10.cloned.1.call-done, u32[]{:T(128)} %bitcast.104), kind=kOutput, calls=%fused_computation.6 | convolution fusion | flops 406585344 | bytes 524800 | tf_op jit(solution)/shard_map/lzfpkq,qx->zfplkx/dot_general | solution.py:35
  377.3 6.5 %convolution_bitcast_fusion = f32[2,1,2,1,32,512]{5,4,2,0,1,3:T(8,128)S(1)} fusion(f32[8,2,1,2,32,512]{5,4,3,0,2,1:T(8,128)} %all-reduce.10.cloned.1.call-done, u32[]{:T(128)} %bitcast.104), kind=kOutput, calls=%fused_computation.5 | convolution fusion | flops 406585344 | bytes 524800 | tf_op jit(solution)/shard_map/lzfpkq,qx->zfplkx/dot_general | solution.py:36
  383.9 0.7 copy.42
  384.6 1.1 reshape.514
  385.7 19.8 %all_to_all.62 = f32[16,1,4096]{2,1,0:T(1,128)S(1)} all-to-all(f32[16,1,4096]{2,1,0:T(1,128)S(1)} %reshape.514), channel_id=1, replica_groups=mesh['freq'=4,'layer'=8,'lat'=16] {'lat'}, dimensions={0} | all-to-all | bytes 524288 | tf_op jit(solution)/shard_map/all_to_all | solution.py:38
  405.5 1.3 reduce.5
  406.8 0.9 reshape.515
  408.8 4.9 fusion.17
  413.7 4.9 fusion.5
  419.5 48.6 %all-reduce.6.cloned.1.call-done = f32[1,32,512]{2,1,0:T(8,128)} async-done(((f32[1,32,512]{2,1,0:T(8,128)}), f32[1,32,512]{2,1,0:T(8,128)}) %all-reduce.6.cloned.1.call-update) | async-done | bytes 65552 | tf_op jit(solution)/shard_map/psum | solution.py:69
  468.2 1.6 fusion.1
  469.8 26.1 %psum.15 = f32[1,8]{1,0:T(1,128)} all-reduce(f32[1,8]{1,0:T(1,128)S(1)} %fusion.1), channel_id=1, replica_groups=mesh['freq'=4,'layer'=8,'lat'=16] {'lat'}, use_global_device_ids=true, to_apply=%region_4.5 | all-reduce | flops 8 | bytes 64 | tf_op jit(solution)/shard_map/psum | solution.py:74
  495.9 1.5 copy.70
  (43 shorter events, 7.2 us)
Async XLA Ops:
  18.9 12.9 %copy-start.1 = (f32[2,1,8,1,32,512]{5,4,3,2,1,0:T(8,128)S(1)}, f32[2,1,8,1,32,512]{5,4,3,2,1,0:T(8,128)}, u32[]{:S(2)}) copy-start(f32[2,1,8,1,32,512]{5,4,3,2,1,0:T(8,128)} %param.7) | copy-start | bytes 3145732
  21.4 21.9 %all-to-all-start = ((f32[16,1,4096]{2,1,0:T(1,128)}), f32[16,1,4096]{2,1,0:T(1,128)S(1)}, u32[]{:S(2)}, u32[]{:S(2)}) async-start(f32[16,1,4096]{2,1,0:T(1,128)} %reshape.508), calls=%async_computation | async-start | bytes 524288 | tf_op jit(solution)/shard_map/all_to_all | solution.py:28
  31.6 140.2 %all-reduce.8.cloned.1.call-start = ((), (), s32[]{:S(2)}) async-start(), calls=%async_computation.5 | async-start | bytes 4194304
  58.8 311.8 %all-reduce.10.cloned.1.call-start = ((), (), s32[]{:S(2)}) async-start(), calls=%async_computation.6 | async-start | bytes 4194304
  214.8 5.0 copy-start
  261.1 207.1 %all-reduce.6.cloned.1.call-start = ((), (), s32[]{:S(2)}) async-start(), calls=%async_computation.4 | async-start | bytes 131072 | tf_op jit(solution)/shard_map/psum | solution.py:69
  413.7 5.1 %copy-start.2 = (f32[2,1,2,1,32,512]{5,4,3,2,1,0:T(8,128)S(1)}, f32[2,1,2,1,32,512]{5,4,3,2,1,0:T(8,128)}, u32[]{:S(2)}) copy-start(f32[2,1,2,1,32,512]{5,4,3,2,1,0:T(8,128)} %param.8) | copy-start | bytes 786436
  418.6 0.8 copy-start.3
Sparse Core Ops, SparseCore 0:
  58.9 112.8 all-reduce.7
  261.2 109.3 all-reduce.9
  419.6 48.5 all-reduce.5
where the time goes:
time: 510 us; the launch traced here: 504 us
  waiting for transfers between devices  281 us (55%)
  matrix products  87.1 us (17%)
  blocking collectives  80.3 us (16%)
  local copies, waits for them, and re-layouts  19.7 us (4%)
  between operations  14.5 us (3%)
  other arithmetic  10.9 us (2%)
  starting transfers between devices  10.7 us (2%)
    unnamed x5, waiting for transfers between devices  221 us
    psum x1, waiting for transfers between devices, per_device(): cell = lax.psum(cell_terms, 'freq')  48.6 us
    all_to_all x2, blocking collectives, inverse(): lax.all_to_all(half_back, 'lat', split_axis=5, concat_axis=4, tiled=True)  39.8 us
    psum x1, blocking collectives, per_device(): classes = lax.psum(local_sums, 'lat')  26.1 us
    all_to_all x1, blocking collectives, forward(): lax.all_to_all(partial_spec, 'lat', split_axis=4, concat_axis=5, tiled=True)  14.4 us
    dot_general x2, matrix products, inverse(): first = jnp.einsum('lzfpkq,qx->zfplkx', mixed, cosine, precision=highest)  13.2 us
    dot_general x2, matrix products, inverse(): second = jnp.einsum('lzfpkq,qx->zfplkx', mixed, sine, precision=highest)  13.1 us
    all_to_all x1, waiting for transfers between devices, forward(): lax.all_to_all(partial_spec, 'lat', split_axis=4, concat_axis=5, tiled=True)  11.4 us
  transfers between devices with their start and end apart: 4, of which 4 were waited for; matrix products, arithmetic and copies ran while one was open for 0% of the time, Pallas kernels for 0%

commit v1 on v0

v1 whole, which is shorter than its diff:
```python
import functools

import jax
import jax.numpy as jnp
import numpy as np
from jax import lax
from jax.experimental import pallas as pl
from jax.experimental.pallas import tpu as pltpu
from jax.sharding import PartitionSpec as P

ITERS = 2
CLASSES = 8
LANES = 128
MESH = pl.DeviceIdType.MESH
F32 = jnp.float32
BF16 = jnp.bfloat16


def tables(length):
    index = np.arange(length)
    angle = (index[:, None] * index[None, :] % length) * (2.0 * np.pi / length)
    both = np.concatenate([np.cos(angle), np.sin(angle)]) / np.sqrt(length)
    high = both.astype(BF16)
    low = (both - high.astype(np.float64)).astype(BF16)
    return high, low


def split(value):
    high = value.astype(BF16)
    return high, (value - high.astype(F32)).astype(BF16)


def dot(a, b):
    return jnp.dot(a, b, preferred_element_type=F32)


def lane_of(shape):
    return lax.broadcasted_iota(jnp.int32, shape, len(shape) - 1)


def turn_lanes(parts):
    lane = lane_of(parts[0].shape)
    odd = (lane // 32) % 2 == 1
    low = lane < 64
    pairs = []
    for first, second in ((parts[0], parts[1]), (parts[2], parts[3])):
        pairs.append(
            (
                jnp.where(odd, pltpu.roll(second, 32, 1), first),
                jnp.where(odd, second, pltpu.roll(first, LANES - 32, 1)),
            )
        )
    (t0, t1), (t2, t3) = pairs
    return (
        jnp.where(low, t0, pltpu.roll(t2, 64, 1)),
        jnp.where(low, t1, pltpu.roll(t3, 64, 1)),
        jnp.where(low, pltpu.roll(t0, 64, 1), t2),
        jnp.where(low, pltpu.roll(t1, 64, 1), t3),
    )


def turned(value, sign):
    real = (lane_of(value.shape) // 32) % 2 == 0
    return jnp.where(real, -sign * pltpu.roll(value, LANES - 32, 1), sign * pltpu.roll(value, 32, 1))


def kernel(
    lat, layers, freqs, n,
    src_hbm, con_hbm, grn_hbm, efd_hbm, cls_hbm, high_hbm, low_hbm,
    cell_out, class_out,
    src, con, grn, efd, cls, high, low,
    field, rows_buf, cols_buf, prod,
    send_a, recv_a, send_b, recv_b, send_c, recv_c, send_d, recv_d,
    send_g, recv_g, wide_g,
    terms, recv_t, cell, part, recv_l, part_f, recv_k,
    load_sem, own_sem,
    sa_sem, ra_sem, sb_sem, rb_sem, sc_sem, rc_sem, sd_sem, rd_sem,
    sg_sem, rg_sem, st_sem, rt_sem, sl_sem, rl_sem, su_sem, ru_sem, sk_sem, rk_sem,
):
    at = {"lat": lax.axis_index("lat"), "layer": lax.axis_index("layer"), "freq": lax.axis_index("freq")}
    size = {"lat": lat, "layer": layers, "freq": freqs}
    wide = n // layers
    groups = 2 * layers // 4

    barrier = pltpu.get_barrier_semaphore()
    for axis in ("lat", "layer", "freq"):
        def greet(k, carry, axis=axis):
            peer = lax.rem(at[axis] + k, size[axis])
            pl.semaphore_signal(barrier, inc=1, device_id={axis: peer}, device_id_type=MESH)
            return carry
        lax.fori_loop(1, size[axis], greet, 0)

    loads = [
        pltpu.make_async_copy(a, b, load_sem.at[i])
        for i, (a, b) in enumerate(
            ((src_hbm, src), (con_hbm, con), (high_hbm, high), (low_hbm, low), (grn_hbm, grn), (efd_hbm, efd), (cls_hbm, cls))
        )
    ]
    for load in loads:
        load.start()

    def remote(axis, peer, source, target, send_sem, recv_sem):
        return pltpu.make_async_remote_copy(
            src_ref=source, dst_ref=target, send_sem=send_sem, recv_sem=recv_sem,
            device_id={axis: peer}, device_id_type=MESH,
        )

    def each_peer(axis, act):
        def one(k, carry):
            act(lax.rem(at[axis] + k, size[axis]))
            return carry
        lax.fori_loop(1, size[axis], one, 0)

    def swap(axis, source, target, rows, send_sem, recv_sem, own):
        me = at[axis]
        def block(ref, i):
            return ref.at[pl.ds(pl.multiple_of(i * rows, 8), rows)]
        def copy(peer, landing):
            return remote(axis, peer, block(source, peer), block(target, landing), send_sem.at[peer], recv_sem.at[landing])
        def mine():
            return pltpu.make_async_copy(block(source, me), block(target, me), own)
        def start():
            each_peer(axis, lambda peer: copy(peer, me).start())
            mine().start()
        def arrived():
            each_peer(axis, lambda peer: copy(peer, peer).wait_recv())
            mine().wait()
        def sent():
            each_peer(axis, lambda peer: copy(peer, me).wait_send())
        return start, arrived, sent

    def spread(axis, source, target, send_sem, recv_sem, own):
        me = at[axis]
        def copy(peer, landing):
            return remote(axis, peer, source, target.at[landing], send_sem.at[peer], recv_sem.at[landing])
        def mine():
            return pltpu.make_async_copy(source, target.at[me], own)
        def start():
            each_peer(axis, lambda peer: copy(peer, me).start())
            mine().start()
        def arrived():
            each_peer(axis, lambda peer: copy(peer, peer).wait_recv())
            mine().wait()
        def sent():
            each_peer(axis, lambda peer: copy(peer, me).wait_send())
        return start, arrived, sent

    green_copies = swap("layer", send_g, recv_g, groups * wide, sg_sem, rg_sem, own_sem.at[8])

    def exchanges(step):
        return (
            swap("lat", send_a.at[step], recv_a.at[step], 32, sa_sem.at[step], ra_sem.at[step], own_sem.at[step * 4]),
            swap("layer", send_b.at[step], recv_b.at[step], wide, sb_sem.at[step], rb_sem.at[step], own_sem.at[step * 4 + 1]),
            swap("layer", send_c.at[step], recv_c.at[step], wide, sc_sem.at[step], rc_sem.at[step], own_sem.at[step * 4 + 2]),
            swap("lat", send_d.at[step], recv_d.at[step], 32, sd_sem.at[step], rd_sem.at[step], own_sem.at[step * 4 + 3]),
        )

    chunk = min(256, n)

    def lane_transform(start, width):
        whole = rows_buf[...]
        upper = rows_buf[0:LANES]
        out = []
        for base in (0, n):
            product = dot(whole, high[base:base + n, start:start + width])
            out.append(product[:LANES] + product[LANES:] + dot(upper, low[base:base + n, start:start + width]))
        return out

    def row_transform(source, target, sign):
        upper, lower = split(source[...])
        cols_buf[:, 0:LANES] = upper
        cols_buf[:, LANES:2 * LANES] = lower
        prod[...] = dot(high[...], cols_buf[...])
        tail = dot(low[...], cols_buf[:, 0:LANES])
        full = prod[:, 0:LANES] + prod[:, LANES:2 * LANES] + tail
        target[...] = full[:n] + turned(full[n:], sign)

    loads[0].wait()
    loads[1].wait()
    field[...] = src[...]
    loads[2].wait()
    loads[3].wait()

    def iterate(step, carry):
        (start_a, came_a, _), (start_b, came_b, _), (start_c, came_c, _), (start_d, came_d, _) = exchanges(step)

        for pol in range(2):
            for piece, value in enumerate(
                (
                    con[0] * field[0, pol] - con[1] * field[1, pol],
                    con[0] * field[1, pol] + con[1] * field[0, pol],
                )
            ):
                row = piece * 64 + pol * 32
                upper, lower = split(value)
                rows_buf[row:row + 32] = upper
                rows_buf[LANES + row:LANES + row + 32] = lower
        for start in range(0, n, chunk):
            cosine, sine = lane_transform(start, chunk)
            real = cosine[:64] + sine[64:]
            imag = cosine[64:] - sine[:64]
            for tile in range(chunk // LANES):
                lanes = slice(tile * LANES, (tile + 1) * LANES)
                blocks = turn_lanes((real[:32, lanes], imag[:32, lanes], real[32:, lanes], imag[32:, lanes]))
                for g, block in enumerate(blocks):
                    row = (start // LANES + tile) * LANES + g * 32
                    send_a[step, row:row + 32] = block

        @pl.when(step == 0)
        def _():
            pl.semaphore_wait(barrier, lat + layers + freqs - 3)

        start_a()

        @pl.when(step == 0)
        def _():
            loads[4].wait()
            for g in range(groups):
                for tile in range(n // LANES):
                    rows = grn[4 * g:4 * g + 4, :, tile * LANES:(tile + 1) * LANES].reshape(LANES, LANES)
                    flipped = rows.T
                    for half in range(LANES // wide):
                        row = ((tile * LANES // wide + half) * groups + g) * wide
                        send_g[row:row + wide] = flipped[half * wide:(half + 1) * wide]
            green_copies[0]()

        came_a()
        row_transform(recv_a.at[step], send_b.at[step], -1.0)
        start_b()

        @pl.when(step == 0)
        def _():
            green_copies[1]()
            def widen(i, carry):
                value = recv_g[pl.ds(pl.multiple_of(i * wide, 8), wide)]
                lane = lane_of(value.shape)
                low_half = lane < 64
                odd = (lane // 32) % 2 == 1
                moved = pltpu.roll(value, 64, 1)
                for pair, double in enumerate((jnp.where(low_half, value, moved), jnp.where(low_half, moved, value))):
                    other = pltpu.roll(double, 32, 1)
                    wide_g[i * 4 + pair * 2] = jnp.where(odd, other, double)
                    wide_g[i * 4 + pair * 2 + 1] = jnp.where(odd, double, other)
                return carry
            lax.fori_loop(0, layers * groups, widen, 0)

        came_b()

        def mix(r, carry):
            base = pl.multiple_of(r * 8, 8)
            sums = [None] * layers
            for l in range(layers):
                value = recv_b[step, pl.ds(pl.multiple_of(l * wide + base, 8), 8)]
                side = turned(value, 1.0)
                for o in range(layers):
                    term = (
                        wide_g[l * 2 * layers + o, pl.ds(base, 8)] * value
                        + wide_g[l * 2 * layers + layers + o, pl.ds(base, 8)] * side
                    )
                    sums[o] = term if l == 0 else sums[o] + term
            for o in range(layers):
                send_c[step, pl.ds(pl.multiple_of(o * wide + base, 8), 8)] = sums[o]
            return carry

        lax.fori_loop(0, wide // 8, mix, 0)
        start_c()
        came_c()
        row_transform(recv_c.at[step], send_d.at[step], 1.0)
        start_d()
        came_d()

        for tile in range(n // LANES):
            blocks = turn_lanes([recv_d[step, tile * LANES + g * 32:tile * LANES + g * 32 + 32] for g in range(4)])
            for q, block in enumerate(blocks):
                pol, piece = q // 2, q % 2
                row = piece * 64 + pol * 32
                upper, lower = split(block)
                rows_buf[row:row + 32, tile * LANES:(tile + 1) * LANES] = upper
                rows_buf[LANES + row:LANES + row + 32, tile * LANES:(tile + 1) * LANES] = lower
        for start in range(0, n, chunk):
            lanes = slice(start, start + chunk)
            cosine, sine = lane_transform(start, chunk)
            real = cosine[:64] - sine[64:]
            imag = cosine[64:] + sine[:64]
            for pol in range(2):
                rows = slice(pol * 32, pol * 32 + 32)
                field[0, pol, :, lanes] = src[0, pol, :, lanes] + con[0, :, lanes] * real[rows] - con[1, :, lanes] * imag[rows]
                field[1, pol, :, lanes] = src[1, pol, :, lanes] + con[0, :, lanes] * imag[rows] + con[1, :, lanes] * real[rows]
        return carry

    lax.fori_loop(0, ITERS, iterate, 0)

    loads[5].wait()
    loads[6].wait()
    total = efd[0, 0] * field[0, 0] - efd[1, 0] * field[1, 0]
    total = total + (efd[0, 1] * field[0, 1] - efd[1, 1] * field[1, 1])
    terms[...] = total
    own_rows = 32 // freqs
    scatter = swap("freq", terms, recv_t, own_rows, st_sem, rt_sem, own_sem.at[9])
    scatter[0]()

    for c in range(CLASSES):
        line = jnp.sum(jnp.where(cls[...] == c, total, 0.0), axis=0, keepdims=True)
        line = sum(line[:, t * LANES:(t + 1) * LANES] for t in range(n // LANES))
        part[c:c + 1] = line
    lat_sums = spread("lat", part, recv_l, sl_sem, rl_sem, own_sem.at[10])
    lat_sums[0]()

    scatter[1]()
    mine = recv_t[0:own_rows]
    for f in range(1, freqs):
        mine = mine + recv_t[f * own_rows:(f + 1) * own_rows]
    own = pl.ds(pl.multiple_of(at["freq"] * own_rows, 8), own_rows)
    cell[own] = mine

    def gather(peer, landing):
        rows = pl.ds(pl.multiple_of(landing * own_rows, 8), own_rows)
        return remote("freq", peer, cell.at[rows], cell.at[rows], su_sem.at[peer], ru_sem.at[landing])

    each_peer("freq", lambda peer: gather(peer, at["freq"]).start())

    lat_sums[1]()
    part_f[...] = jnp.sum(recv_l[...], axis=0)
    freq_sums = spread("freq", part_f, recv_k, sk_sem, rk_sem, own_sem.at[11])
    freq_sums[0]()

    each_peer("freq", lambda peer: gather(peer, peer).wait_recv())
    cell_out[...] = cell[...]
    freq_sums[1]()
    sums = jnp.sum(jnp.sum(recv_k[...], axis=0), axis=1, keepdims=True) / float(n)
    spot = lax.broadcasted_iota(jnp.int32, (CLASSES, LANES), 0) == lane_of((CLASSES, LANES))
    class_out[...] = jnp.sum(jnp.where(spot, sums, 0.0), axis=0, keepdims=True)[:, :CLASSES]

    def drain(step, carry):
        for exchange in exchanges(step):
            exchange[2]()
        return carry

    lax.fori_loop(0, ITERS, drain, 0)
    green_copies[2]()
    scatter[2]()
    lat_sums[2]()
    each_peer("freq", lambda peer: gather(peer, at["freq"]).wait_send())
    freq_sums[2]()


def per_device(lat, layers, freqs, source, contrast, green, efield, cell_class):
    n = source.shape[5]
    high, low = tables(n)
    wide = n // layers
    own_rows = 32 // freqs
    dma = pltpu.SemaphoreType.DMA
    stage = pltpu.VMEM((ITERS, n, LANES), F32)
    scratch = [
        pltpu.VMEM((2, 2, 32, n), F32),
        pltpu.VMEM((2, 32, n), F32),
        pltpu.VMEM((2 * layers, 32, n), F32),
        pltpu.VMEM((2, 2, 32, n), F32),
        pltpu.VMEM((32, n), jnp.int32),
        pltpu.VMEM((2 * n, n), BF16),
        pltpu.VMEM((2 * n, n), BF16),
        pltpu.VMEM((2, 2, 32, n), F32),
        pltpu.VMEM((2 * LANES, n), BF16),
        pltpu.VMEM((n, 2 * LANES), BF16),
        pltpu.VMEM((2 * n, 2 * LANES), F32),
        *[stage] * 8,
        pltpu.VMEM((layers * n // 2, LANES), F32),
        pltpu.VMEM((layers * n // 2, LANES), F32),
        pltpu.VMEM((layers * 2 * layers, wide, LANES), F32),
        pltpu.VMEM((32, n), F32),
        pltpu.VMEM((32, n), F32),
        pltpu.VMEM((32, n), F32),
        pltpu.VMEM((CLASSES, LANES), F32),
        pltpu.VMEM((lat, CLASSES, LANES), F32),
        pltpu.VMEM((CLASSES, LANES), F32),
        pltpu.VMEM((freqs, CLASSES, LANES), F32),
        dma((7,)),
        dma((12,)),
        *[dma((ITERS, lat))] * 2,
        *[dma((ITERS, layers))] * 4,
        *[dma((ITERS, lat))] * 2,
        *[dma((layers,))] * 2,
        *[dma((freqs,))] * 2,
        *[dma((lat,))] * 2,
        *[dma((freqs,))] * 4,
    ]
    cell, classes = pl.pallas_call(
        functools.partial(kernel, lat, layers, freqs, n),
        out_shape=(jax.ShapeDtypeStruct((32, n), F32), jax.ShapeDtypeStruct((1, CLASSES), F32)),
        in_specs=[pl.BlockSpec(memory_space=pl.ANY)] * 7,
        out_specs=(pl.BlockSpec(memory_space=pltpu.VMEM), pl.BlockSpec(memory_space=pltpu.VMEM)),
        scratch_shapes=scratch,
        compiler_params=pltpu.CompilerParams(
            collective_id=0, has_side_effects=True, vmem_limit_bytes=48 * 1024 * 1024
        ),
    )(
        source.reshape(2, 2, 32, n),
        contrast.reshape(2, 32, n),
        green.reshape(2 * layers, 32, n),
        efield.reshape(2, 2, 32, n),
        cell_class.reshape(32, n),
        jnp.asarray(high),
        jnp.asarray(low),
    )
    return cell.reshape(1, 32, n), classes


def solution(mesh):
    placed = (
        P(None, "freq", None, "layer", "lat", None),
        P(None, "freq", "layer", "lat", None),
        P(None, "freq", None, "layer", "lat", None),
        P(None, "freq", None, "layer", "lat", None),
        P("layer", "lat", None),
    )
    sizes = (mesh.shape["lat"], mesh.shape["layer"], mesh.shape["freq"])
    return jax.shard_map(
        functools.partial(per_device, *sizes),
        mesh=mesh,
        in_specs=placed,
        out_specs=(P("layer", "lat", None), P("layer", None)),
        check_vma=False,
    )
```

time: 510 us -> 105 us (0.21); the launches traced: 504 us -> 105 us
  waiting for transfers between devices: 281 us -> 0 us
  Pallas kernels: 0 us -> 95.4 us
  matrix products: 87.1 us -> 0 us
  blocking collectives: 80.3 us -> 0 us
  between operations: 14.5 us -> 0.65 us
  local copies, waits for them, and re-layouts: 19.7 us -> 8.45 us
  other arithmetic: 10.9 us -> 0 us
  starting transfers between devices: 10.7 us -> 0 us
    unnamed x5 -> x0, waiting for transfers between devices: 221 us -> none
    pallas_call x0 -> x1, Pallas kernels: none -> 95.4 us  [per_device(): pl.pallas_call(functools.partial(kernel, lat, layers, freqs, n), out_shap...]
    dot_general x17 -> x0, matrix products: 87.1 us -> none  [the longest x2 13.2 us: inverse(): first = jnp.einsum('lzfpkq,qx->zfplkx', mixed, cosine, precision=highest)]
    all_to_all x3 -> x0, blocking collectives: 54.2 us -> none  [the longest x2 39.8 us: inverse(): lax.all_to_all(half_back, 'lat', split_axis=5, concat_axis=4, tiled=True)]
    psum x1 -> x0, waiting for transfers between devices: 48.6 us -> none  [per_device(): cell = lax.psum(cell_terms, 'freq')]
    psum x1 -> x0, blocking collectives: 26.1 us -> none  [per_device(): classes = lax.psum(local_sums, 'lat')]
    all_to_all x1 -> x0, waiting for transfers between devices: 11.4 us -> none  [forward(): lax.all_to_all(partial_spec, 'lat', split_axis=4, concat_axis=5, tiled=True)]
    all_to_all x1 -> x0, starting transfers between devices: 10.2 us -> none  [forward(): lax.all_to_all(partial_spec, 'lat', split_axis=4, concat_axis=5, tiled=True)]
  transfers between devices with their start and end apart: 4 -> 0, of which waited for: 4 -> 0; matrix products, arithmetic and copies ran while one was open for 0% -> 0% of each run, Pallas kernels for 0% -> 0%
where the time goes in v1:
time: 105 us
  Pallas kernels  95.4 us (91%)
  local copies, waits for them, and re-layouts  8.45 us (8%)
    pallas_call x1, Pallas kernels, per_device(): pl.pallas_call(functools.partial(kernel, lat, layers, freqs, n), out_shap...  95.4 us
    unnamed x16, local copies, waits for them, and re-layouts  8.45 us

profile of v1, /device:TPU:1, one launch (start us, length us, event | category | flops | bytes accessed | tf_op | source)
XLA Modules:
  0.0 104.5 jit_solution(1340385773983992063)
XLA Ops:
  0.6 0.0 copy-start
  0.6 1.2 %copy-done = f32[2,1,8,1,32,512]{5,4,3,2,1,0:T(8,128)S(1)} copy-done((f32[2,1,8,1,32,512]{5,4,3,2,1,0:T(8,128)S(1)}, f32[2,1,8,1,32,512]{5,4,3,2,1,0:T(8,128)}, u32[]{:S(2)}) %copy-start) | copy-done | bytes 1048600
  1.9 0.0 copy-start.1
  1.9 1.2 %copy-done.1 = bf16[1024,512]{1,0:T(8,128)(2,1)S(1)} copy-done((bf16[1024,512]{1,0:T(8,128)(2,1)S(1)}, bf16[1024,512]{1,0:T(8,128)(2,1)}, u32[]{:S(2)}) %copy-start.1) | copy-done | bytes 1048600
  3.1 0.0 copy-start.2
  3.1 1.2 %copy-done.2 = bf16[1024,512]{1,0:T(8,128)(2,1)S(1)} copy-done((bf16[1024,512]{1,0:T(8,128)(2,1)S(1)}, bf16[1024,512]{1,0:T(8,128)(2,1)}, u32[]{:S(2)}) %copy-start.2) | copy-done | bytes 1048600
  4.3 0.0 copy-start.3
  4.3 0.9 copy-done.3
  5.3 0.0 copy-start.4
  5.3 0.9 copy-done.4
  6.2 0.0 copy-start.5
  6.2 0.9 copy-done.5
  7.1 0.0 copy-start.6
  7.1 0.8 copy-done.6
  8.0 95.4 %shard_map.86 = (f32[32,512]{1,0:T(8,128)S(1)}, f32[1,8]{1,0:T(1,128)S(1)}) custom-call(f32[2,2,32,512]{3,2,1,0:T(8,128)S(1)} %bitcast.7, f32[2,32,512]{2,1,0:T(8,128)S(1)} %bitcast.9, f32[16,32,512]{2,1,0:T(8,128)S(1)} %bitcast.6, f32[2,2,32,512]{3,2,1,0:T(8,128)S(1)} %bitcast.8, s32[32,512]{1,0:T(8,128)S(1)} %bitcast.10, bf16[1024,512]{1,0:T(8,128)(2,1)S(1)} %copy-done.2, ...), custom_call_target="tpu_custom_call" | custom-call | tf_op jit(solution)/shard_map/pallas_call | solution.py:387
  103.4 0.6 copy.11
  104.0 0.5 copy.12
Async XLA Ops:
  0.6 1.2 %copy-start = (f32[2,1,8,1,32,512]{5,4,3,2,1,0:T(8,128)S(1)}, f32[2,1,8,1,32,512]{5,4,3,2,1,0:T(8,128)}, u32[]{:S(2)}) copy-start(f32[2,1,8,1,32,512]{5,4,3,2,1,0:T(8,128)} %param.9) | copy-start | bytes 3145732
  1.9 1.2 %copy-start.1 = (bf16[1024,512]{1,0:T(8,128)(2,1)S(1)}, bf16[1024,512]{1,0:T(8,128)(2,1)}, u32[]{:S(2)}) copy-start(bf16[1024,512]{1,0:T(8,128)(2,1)} %constant.5.clone.low_hbm) | copy-start | bytes 3145732
  3.1 1.2 %copy-start.2 = (bf16[1024,512]{1,0:T(8,128)(2,1)S(1)}, bf16[1024,512]{1,0:T(8,128)(2,1)}, u32[]{:S(2)}) copy-start(bf16[1024,512]{1,0:T(8,128)(2,1)} %constant.4.clone.high_hbm) | copy-start | bytes 3145732
  4.3 0.9 copy-start.3
  5.3 0.9 copy-start.4
  6.2 0.9 copy-start.5
  7.1 0.8 copy-start.6

commit v2 on v1

--- a/solution.py
+++ b/solution.py
@@ -106,10 +106,16 @@
         )
 
     def each_peer(axis, act):
+        pair = 1 if axis == "freq" else 2
+        ring = size[axis] // pair
         def one(k, carry):
-            act(lax.rem(at[axis] + k, size[axis]))
+            i = k // pair
+            ahead = i % 2
+            hop = ahead * (ring // 2 - (i + 1) // 2) + (1 - ahead) * (ring - ring // 2 + i // 2)
+            place = lax.rem(at[axis] // pair + hop, ring)
+            act(place * pair + (at[axis] + pair - 1 - k % pair) % pair)
             return carry
-        lax.fori_loop(1, size[axis], one, 0)
+        lax.fori_loop(0, size[axis] - 1, one, 0)
 
     def swap(axis, source, target, rows, send_sem, recv_sem, own):
         me = at[axis]
@@ -208,12 +214,6 @@
 
         @pl.when(step == 0)
         def _():
-            pl.semaphore_wait(barrier, lat + layers + freqs - 3)
-
-        start_a()
-
-        @pl.when(step == 0)
-        def _():
             loads[4].wait()
             for g in range(groups):
                 for tile in range(n // LANES):
@@ -222,6 +222,12 @@
                     for half in range(LANES // wide):
                         row = ((tile * LANES // wide + half) * groups + g) * wide
                         send_g[row:row + wide] = flipped[half * wide:(half + 1) * wide]
+            pl.semaphore_wait(barrier, lat + layers + freqs - 3)
+
+        start_a()
+
+        @pl.when(step == 0)
+        def _():
             green_copies[0]()
 
         came_a()
@@ -391,7 +397,7 @@
         out_specs=(pl.BlockSpec(memory_space=pltpu.VMEM), pl.BlockSpec(memory_space=pltpu.VMEM)),
         scratch_shapes=scratch,
         compiler_params=pltpu.CompilerParams(
-            collective_id=0, has_side_effects=True, vmem_limit_bytes=48 * 1024 * 1024
+            collective_id=0, has_side_effects=True
         ),
     )(
         source.reshape(2, 2, 32, n),

time: 105 us -> 96.2 us (0.916)
  local copies, waits for them, and re-layouts: 8.45 us -> 1.99 us
  Pallas kernels: 95.4 us -> 93.1 us
    unnamed x16 -> x4, local copies, waits for them, and re-layouts: 8.45 us -> 1.99 us
    pallas_call x1, Pallas kernels: 95.4 us -> 93.1 us  [per_device(): pl.pallas_call(functools.partial(kernel, lat, layers, freqs, n), out_shap...]
where the time goes in v2:
time: 96.2 us; the launch traced here: 95.7 us
  Pallas kernels  93.1 us (97%)
  local copies, waits for them, and re-layouts  1.99 us (2%)
    pallas_call x1, Pallas kernels, per_device(): pl.pallas_call(functools.partial(kernel, lat, layers, freqs, n), out_shap...  93.1 us
    unnamed x4, local copies, waits for them, and re-layouts  1.99 us

profile of v2, /device:TPU:1, one launch (start us, length us, event | category | flops | bytes accessed | tf_op | source)
XLA Modules:
  0.0 95.7 jit_solution(5824068636327640553)
XLA Ops:
  0.6 93.1 %shard_map.86 = (f32[32,512]{1,0:T(8,128)}, f32[1,8]{1,0:T(1,128)}) custom-call(f32[2,2,32,512]{3,2,1,0:T(8,128)} %bitcast.7, f32[2,32,512]{2,1,0:T(8,128)} %bitcast.9, f32[16,32,512]{2,1,0:T(8,128)} %bitcast.6, f32[2,2,32,512]{3,2,1,0:T(8,128)} %bitcast.8, s32[32,512]{1,0:T(8,128)} %bitcast.10, bf16[1024,512]{1,0:T(8,128)(2,1)} %constant.4.clone.high_hbm, ...), custom_call_target="tpu_custom_call" | custom-call | tf_op jit(solution)/shard_map/pallas_call | solution.py:393
  93.7 0.0 copy-start
  93.7 1.5 %copy.11 = f32[1,32,512]{2,1,0:T(8,128)} copy(f32[1,32,512]{2,1,0:T(8,128)} %bitcast.11) | data formatting | bytes 131072
  95.2 0.0 copy-done
  95.2 0.5 copy.12
Async XLA Ops:
  93.7 1.5 %copy-start = (f32[1,8]{1,0:T(1,128)S(1)}, f32[1,8]{1,0:T(1,128)}, u32[]{:S(2)}) copy-start(f32[1,8]{1,0:T(1,128)} %get-tuple-element.9) | copy-start | bytes 100

commit v3 on v2

v3 whole, which is shorter than its diff:
```python
import functools
import itertools

import jax
import jax.numpy as jnp
import numpy as np
from jax import lax
from jax.experimental import pallas as pl
from jax.experimental.pallas import tpu as pltpu
from jax.sharding import PartitionSpec as P

ITERS = 2
CLASSES = 8
LANES = 128
MESH = pl.DeviceIdType.MESH
F32 = jnp.float32
BF16 = jnp.bfloat16


def tables(length):
    half = np.arange(length // 2)
    phases = (2 * half[:, None] * half[None, :], half[:, None] * (2 * half[None, :] + 1), (2 * half[:, None] + 1) * half[None, :])
    angles = [(phase % length) * (2.0 * np.pi / length) for phase in phases]
    both = np.stack([np.concatenate([np.cos(angle), np.sin(angle)]) for angle in angles]) / np.sqrt(length)
    high = both.astype(BF16)
    low = (both - high.astype(np.float64)).astype(BF16)
    return high, low


def split(value):
    high = value.astype(BF16)
    return high, (value - high.astype(F32)).astype(BF16)


def dot(a, b):
    return jnp.dot(a, b, preferred_element_type=F32)


def lane_of(shape):
    return lax.broadcasted_iota(jnp.int32, shape, len(shape) - 1)


def turn_lanes(parts):
    parts = list(parts)
    lane = lane_of(parts[0].shape)
    for bit in (1, 2, 4):
        width = 16 * bit
        odd = (lane // width) % 2 == 1
        for q in range(8):
            if q & bit == 0:
                first, second = parts[q], parts[q | bit]
                parts[q] = jnp.where(odd, pltpu.roll(second, width, 1), first)
                parts[q | bit] = jnp.where(odd, second, pltpu.roll(first, LANES - width, 1))
    return parts


def turned(value, sign):
    real = (lane_of(value.shape) // 32) % 2 == 0
    return jnp.where(real, -sign * pltpu.roll(value, LANES - 32, 1), sign * pltpu.roll(value, 32, 1))


def butterfly(value):
    return pltpu.roll(value, 64, 1) + jnp.where(lane_of(value.shape) < 64, value, -value)


def kernel(
    lat, layers, freqs, n,
    src_hbm, con_hbm, grn_hbm, efd_hbm, cls_hbm, high_hbm, low_hbm,
    cell_out, class_out,
    src_raw, con_raw, grn, efd, cls, high, low,
    src, con, field, rows_buf, cols_buf, prod,
    send_a, recv_a, send_b, recv_b, send_c, recv_c, send_d, recv_d,
    send_g, recv_g, wide_g,
    terms, recv_t, cell, part, recv_l, part_f, recv_k,
    load_sem, own_sem,
    sa_sem, ra_sem, sb_sem, rb_sem, sc_sem, rc_sem, sd_sem, rd_sem,
    sg_sem, rg_sem, st_sem, rt_sem, sl_sem, rl_sem, su_sem, ru_sem, sk_sem, rk_sem,
):
    at = {"lat": lax.axis_index("lat"), "layer": lax.axis_index("layer"), "freq": lax.axis_index("freq")}
    size = {"lat": lat, "layer": layers, "freq": freqs}
    half = n // 2
    wide = half // layers

    barrier = pltpu.get_barrier_semaphore()
    for axis in ("lat", "layer", "freq"):
        def greet(k, carry, axis=axis):
            peer = lax.rem(at[axis] + k, size[axis])
            pl.semaphore_signal(barrier, inc=1, device_id={axis: peer}, device_id_type=MESH)
            return carry
        lax.fori_loop(1, size[axis], greet, 0)

    tiles = n // LANES

    def by_tile(i, source, target):
        lead = (slice(None),) * (len(source.shape) - 1)
        return [
            pltpu.make_async_copy(source.at[lead + (slice(t * LANES, (t + 1) * LANES),)], target.at[t], load_sem.at[i, t])
            for t in range(tiles)
        ]

    loads = [
        by_tile(0, src_hbm, src_raw),
        by_tile(1, con_hbm, con_raw),
        [pltpu.make_async_copy(high_hbm, high, load_sem.at[2, 0])],
        [pltpu.make_async_copy(low_hbm, low, load_sem.at[3, 0])],
        by_tile(4, grn_hbm, grn),
        by_tile(5, efd_hbm, efd),
        [pltpu.make_async_copy(cls_hbm, cls, load_sem.at[6, 0])],
    ]
    for load in loads:
        for copy in load:
            copy.start()

    def loaded(i):
        for copy in loads[i]:
            copy.wait()

    def remote(axis, peer, source, target, send_sem, recv_sem):
        return pltpu.make_async_remote_copy(
            src_ref=source, dst_ref=target, send_sem=send_sem, recv_sem=recv_sem,
            device_id={axis: peer}, device_id_type=MESH,
        )

    def each_peer(axis, act):
        pair = 1 if axis == "freq" else 2
        ring = size[axis] // pair
        def one(k, carry):
            i = k // pair
            ahead = i % 2
            hop = ahead * (ring // 2 - (i + 1) // 2) + (1 - ahead) * (ring - ring // 2 + i // 2)
            place = lax.rem(at[axis] // pair + hop, ring)
            act(place * pair + (at[axis] + pair - 1 - k % pair) % pair)
            return carry
        lax.fori_loop(0, size[axis] - 1, one, 0)

    def swap(axis, source, target, rows, send_sem, recv_sem, own):
        me = at[axis]
        def block(ref, i):
            return ref.at[pl.ds(pl.multiple_of(i * rows, 8), rows)]
        def copy(peer, landing):
            return remote(axis, peer, block(source, peer), block(target, landing), send_sem.at[peer], recv_sem.at[landing])
        def mine():
            return pltpu.make_async_copy(block(source, me), block(target, me), own)
        def start():
            each_peer(axis, lambda peer: copy(peer, me).start())
            mine().start()
        def arrived():
            each_peer(axis, lambda peer: copy(peer, peer).wait_recv())
            mine().wait()
        def sent():
            each_peer(axis, lambda peer: copy(peer, me).wait_send())
        return start, arrived, sent

    def spread(axis, source, target, send_sem, recv_sem, own):
        me = at[axis]
        def copy(peer, landing):
            return remote(axis, peer, source, target.at[landing], send_sem.at[peer], recv_sem.at[landing])
        def mine():
            return pltpu.make_async_copy(source, target.at[me], own)
        def start():
            each_peer(axis, lambda peer: copy(peer, me).start())
            mine().start()
        def arrived():
            each_peer(axis, lambda peer: copy(peer, peer).wait_recv())
            mine().wait()
        def sent():
            each_peer(axis, lambda peer: copy(peer, me).wait_send())
        return start, arrived, sent

    green_copies = swap("layer", send_g, recv_g, half, sg_sem, rg_sem, own_sem.at[16])

    def exchange(which, step, pol):
        axis, source, target, rows, send_sem, recv_sem = (
            ("lat", send_a, recv_a, 16, sa_sem, ra_sem),
            ("layer", send_b, recv_b, wide, sb_sem, rb_sem),
            ("layer", send_c, recv_c, wide, sc_sem, rc_sem),
            ("lat", send_d, recv_d, 16, sd_sem, rd_sem),
        )[which]
        return swap(
            axis, source.at[step, pol], target.at[step, pol], rows, send_sem.at[step, pol], recv_sem.at[step, pol],
            own_sem.at[(step * 2 + pol) * 4 + which],
        )

    def lane_transform(parity, table):
        whole = rows_buf[parity]
        upper = rows_buf[parity, 0:64]
        out = []
        for base in (0, half):
            product = dot(whole, high[table, base:base + half])
            out.append(product[:64] + product[64:] + dot(upper, low[table, base:base + half]))
        return out

    def row_transform(value, odd_table):
        upper, lower = split(value)
        cols_buf[:, 0:LANES] = upper
        cols_buf[:, LANES:2 * LANES] = lower
        for i, table in enumerate((0, odd_table)):
            prod[i] = dot(high[table], cols_buf[...])
        full = []
        for i, table in enumerate((0, odd_table)):
            tail = dot(low[table], cols_buf[:, 0:LANES])
            full.append(prod[i, :, 0:LANES] + prod[i, :, LANES:2 * LANES] + tail)
        both = jnp.where(lane_of(full[0].shape) < 64, full[0], full[1])
        return both[:half], both[half:]

    def put_rows(parity, row, lanes, value):
        upper, lower = split(value)
        count = value.shape[0]
        rows_buf[parity, row:row + count, lanes] = upper
        rows_buf[parity, 64 + row:64 + row + count, lanes] = lower

    def forward_lanes(step, pol):
        for piece, value in enumerate(
            (
                con[0] * field[0, pol] - con[1] * field[1, pol],
                con[0] * field[1, pol] + con[1] * field[0, pol],
            )
        ):
            put_rows(0, piece * 32, slice(None), value[:, :half] + value[:, half:])
            put_rows(1, piece * 32, slice(None), value[:, :half] - value[:, half:])
        pieces = []
        for parity in range(2):
            cosine, sine = lane_transform(parity, parity)
            pieces.append((cosine[:32] + sine[32:], cosine[32:] - sine[:32]))
        for tile in range(half // LANES):
            lanes = slice(tile * LANES, (tile + 1) * LANES)
            blocks = turn_lanes(
                [pieces[q % 2][q // 2 % 2][q // 4 * 16:q // 4 * 16 + 16, lanes] for q in range(8)]
            )
            for g, block in enumerate(blocks):
                row = (tile * 8 + g) * 16
                send_a[step, pol, row:row + 16] = block

    def inverse_lanes(step, pol):
        for tile in range(half // LANES):
            lanes = slice(tile * LANES, (tile + 1) * LANES)
            blocks = turn_lanes([recv_d[step, pol, pl.ds((tile * 8 + g) * 16, 16)] for g in range(8)])
            for q, block in enumerate(blocks):
                put_rows(q % 2, q // 2 % 2 * 32 + q // 4 * 16, lanes, block)
        pieces = []
        for parity in range(2):
            cosine, sine = lane_transform(parity, 2 * parity)
            pieces.append((cosine[:32] - sine[32:], cosine[32:] + sine[:32]))
        for lanes, sign in ((slice(0, half), 1.0), (slice(half, n), -1.0)):
            real, imag = (pieces[0][i] + sign * pieces[1][i] for i in range(2))
            field[0, pol, :, lanes] = src[0, pol, :, lanes] + con[0, :, lanes] * real - con[1, :, lanes] * imag
            field[1, pol, :, lanes] = src[1, pol, :, lanes] + con[0, :, lanes] * imag + con[1, :, lanes] * real

    def prepare_green():
        loaded(4)
        for pair in range(layers):
            for tile in range(half // LANES):
                rows = [
                    grn[end * (half // LANES) + tile, 2 * pair + s, pl.ds(parity, 16, stride=2)]
                    for end in range(2) for s in range(2) for parity in range(2)
                ]
                flipped = jnp.concatenate(rows, axis=0).T
                for part_of in range(LANES // wide):
                    row = ((tile * LANES // wide + part_of) * layers + pair) * wide
                    send_g[row:row + wide] = flipped[part_of * wide:(part_of + 1) * wide]

    def widen(i, carry):
        value = recv_g[pl.ds(pl.multiple_of(i * wide, 8), wide)]
        odd = (lane_of(value.shape) // 32) % 2 == 1
        wide_g[i * 2] = jnp.where(odd, pltpu.roll(value, 32, 1), value)
        wide_g[i * 2 + 1] = jnp.where(odd, value, pltpu.roll(value, LANES - 32, 1))
        return carry

    def mix(step, pol):
        def rows(r, carry):
            base = pl.multiple_of(r * 8, 8)
            sums = [None] * layers
            for l in range(layers):
                value = recv_b[step, pol, pl.ds(pl.multiple_of(l * wide + base, 8), 8)]
                side = turned(value, 1.0)
                for o in range(layers):
                    term = (
                        wide_g[l * 2 * layers + o, pl.ds(base, 8)] * value
                        + wide_g[l * 2 * layers + layers + o, pl.ds(base, 8)] * side
                    )
                    sums[o] = term if l == 0 else sums[o] + term
            for o in range(layers):
                send_c[step, pol, pl.ds(pl.multiple_of(o * wide + base, 8), 8)] = sums[o]
            return carry

        lax.fori_loop(0, wide // 8, rows, 0)

    even_odd = [(slice(parity * 16, parity * 16 + 16), pl.ds(parity, 16, stride=2)) for parity in range(2)]
    loaded(1)
    for mine, stride in even_odd:
        for piece, t in itertools.product(range(2), range(tiles)):
            con[piece, mine, t * LANES:(t + 1) * LANES] = con_raw[t, piece, stride]
    loaded(0)
    for mine, stride in even_odd:
        for piece, pol, t in itertools.product(range(2), range(2), range(tiles)):
            value = src_raw[t, piece, pol, stride]
            src[piece, pol, mine, t * LANES:(t + 1) * LANES] = value
            field[piece, pol, mine, t * LANES:(t + 1) * LANES] = value
    loaded(2)
    loaded(3)

    def iterate(step, carry):
        for pol in range(2):
            @pl.when(step > 0)
            def _():
                exchange(3, step - 1, pol)[1]()
                inverse_lanes(step - 1, pol)

            forward_lanes(step, pol)

            if pol == 0:
                @pl.when(step == 0)
                def _():
                    pl.semaphore_wait(barrier, lat + layers + freqs - 3)

            exchange(0, step, pol)[0]()

        @pl.when(step == 0)
        def _():
            prepare_green()
            green_copies[0]()

        for pol in range(2):
            exchange(0, step, pol)[1]()
            cosine, sine = row_transform(recv_a[step, pol], 1)
            send_b[step, pol] = butterfly(cosine + turned(sine, -1.0))
            exchange(1, step, pol)[0]()

        @pl.when(step == 0)
        def _():
            green_copies[1]()
            lax.fori_loop(0, layers * layers, widen, 0)

        for pol in range(2):
            exchange(1, step, pol)[1]()
            mix(step, pol)
            exchange(2, step, pol)[0]()

        for pol in range(2):
            exchange(2, step, pol)[1]()
            cosine, sine = row_transform(butterfly(recv_c[step, pol]), 2)
            send_d[step, pol] = cosine + turned(sine, 1.0)
            exchange(3, step, pol)[0]()
        return carry

    lax.fori_loop(0, ITERS, iterate, 0)

    loaded(5)
    loaded(6)
    for pol in range(2):
        exchange(3, ITERS - 1, pol)[1]()
        inverse_lanes(ITERS - 1, pol)
        for parity, t in itertools.product(range(2), range(tiles)):
            mine = slice(parity * 16, parity * 16 + 16)
            lanes = slice(t * LANES, (t + 1) * LANES)
            stride = pl.ds(parity, 16, stride=2)
            value = efd[t, 0, pol, stride] * field[0, pol, mine, lanes] - efd[t, 1, pol, stride] * field[1, pol, mine, lanes]
            spots = pl.ds(t * 32 + parity, 16, stride=2)
            terms[spots] = value if pol == 0 else terms[spots] + value
    own_rows = tiles * 32 // freqs
    scatter = swap("freq", terms, recv_t, own_rows, st_sem, rt_sem, own_sem.at[17])
    scatter[0]()

    for c in range(CLASSES):
        kept = [
            jnp.where(cls[:, t * LANES:(t + 1) * LANES] == c, terms[t * 32:(t + 1) * 32], 0.0) for t in range(tiles)
        ]
        part[c:c + 1] = jnp.sum(sum(kept), axis=0, keepdims=True)
    lat_sums = spread("lat", part, recv_l, sl_sem, rl_sem, own_sem.at[18])
    lat_sums[0]()

    scatter[1]()
    mine = recv_t[0:own_rows]
    for f in range(1, freqs):
        mine = mine + recv_t[f * own_rows:(f + 1) * own_rows]
    own = pl.ds(pl.multiple_of(at["freq"] * own_rows, 8), own_rows)
    cell[own] = mine

    def gather(peer, landing):
        rows = pl.ds(pl.multiple_of(landing * own_rows, 8), own_rows)
        return remote("freq", peer, cell.at[rows], cell.at[rows], su_sem.at[peer], ru_sem.at[landing])

    each_peer("freq", lambda peer: gather(peer, at["freq"]).start())

    lat_sums[1]()
    part_f[...] = jnp.sum(recv_l[...], axis=0)
    freq_sums = spread("freq", part_f, recv_k, sk_sem, rk_sem, own_sem.at[19])
    freq_sums[0]()

    each_peer("freq", lambda peer: gather(peer, peer).wait_recv())
    for t in range(tiles):
        cell_out[:, t * LANES:(t + 1) * LANES] = cell[t * 32:(t + 1) * 32]
    freq_sums[1]()
    sums = jnp.sum(jnp.sum(recv_k[...], axis=0), axis=1, keepdims=True) / float(n)
    spot = lax.broadcasted_iota(jnp.int32, (CLASSES, LANES), 0) == lane_of((CLASSES, LANES))
    class_out[...] = jnp.sum(jnp.where(spot, sums, 0.0), axis=0, keepdims=True)[:, :CLASSES]

    def drain(step, carry):
        for pol in range(2):
            for which in range(4):
                exchange(which, step, pol)[2]()
        return carry

    lax.fori_loop(0, ITERS, drain, 0)
    green_copies[2]()
    scatter[2]()
    lat_sums[2]()
    each_peer("freq", lambda peer: gather(peer, at["freq"]).wait_send())
    freq_sums[2]()


def per_device(lat, layers, freqs, source, contrast, green, efield, cell_class):
    n = source.shape[5]
    high, low = tables(n)
    half = n // 2
    wide = half // layers
    dma = pltpu.SemaphoreType.DMA
    stage = pltpu.VMEM((ITERS, 2, half, LANES), F32)
    tiles = n // LANES
    scratch = [
        pltpu.VMEM((tiles, 2, 2, 32, LANES), F32),
        pltpu.VMEM((tiles, 2, 32, LANES), F32),
        pltpu.VMEM((tiles, 2 * layers, 32, LANES), F32),
        pltpu.VMEM((tiles, 2, 2, 32, LANES), F32),
        pltpu.VMEM((32, n), jnp.int32),
        pltpu.VMEM((3, n, half), BF16),
        pltpu.VMEM((3, n, half), BF16),
        pltpu.VMEM((2, 2, 32, n), F32),
        pltpu.VMEM((2, 32, n), F32),
        pltpu.VMEM((2, 2, 32, n), F32),
        pltpu.VMEM((2, LANES, half), BF16),
        pltpu.VMEM((half, 2 * LANES), BF16),
        pltpu.VMEM((2, n, 2 * LANES), F32),
        *[stage] * 8,
        pltpu.VMEM((layers * half, LANES), F32),
        pltpu.VMEM((layers * half, LANES), F32),
        pltpu.VMEM((layers * 2 * layers, wide, LANES), F32),
        pltpu.VMEM((tiles * 32, LANES), F32),
        pltpu.VMEM((tiles * 32, LANES), F32),
        pltpu.VMEM((tiles * 32, LANES), F32),
        pltpu.VMEM((CLASSES, LANES), F32),
        pltpu.VMEM((lat, CLASSES, LANES), F32),
        pltpu.VMEM((CLASSES, LANES), F32),
        pltpu.VMEM((freqs, CLASSES, LANES), F32),
        dma((7, tiles)),
        dma((20,)),
        *[dma((ITERS, 2, lat))] * 2,
        *[dma((ITERS, 2, layers))] * 4,
        *[dma((ITERS, 2, lat))] * 2,
        *[dma((layers,))] * 2,
        *[dma((freqs,))] * 2,
        *[dma((lat,))] * 2,
        *[dma((freqs,))] * 4,
    ]
    cell, classes = pl.pallas_call(
        functools.partial(kernel, lat, layers, freqs, n),
        out_shape=(jax.ShapeDtypeStruct((32, n), F32), jax.ShapeDtypeStruct((1, CLASSES), F32)),
        in_specs=[pl.BlockSpec(memory_space=pl.ANY)] * 7,
        out_specs=(pl.BlockSpec(memory_space=pltpu.VMEM), pl.BlockSpec(memory_space=pltpu.VMEM)),
        scratch_shapes=scratch,
        compiler_params=pltpu.CompilerParams(
            collective_id=0, has_side_effects=True
        ),
    )(
        source.reshape(2, 2, 32, n),
        contrast.reshape(2, 32, n),
        green.reshape(2 * layers, 32, n),
        efield.reshape(2, 2, 32, n),
        cell_class.reshape(32, n),
        jnp.asarray(high),
        jnp.asarray(low),
    )
    return cell.reshape(1, 32, n), classes


def solution(mesh):
    placed = (
        P(None, "freq", None, "layer", "lat", None),
        P(None, "freq", "layer", "lat", None),
        P(None, "freq", None, "layer", "lat", None),
        P(None, "freq", None, "layer", "lat", None),
        P("layer", "lat", None),
    )
    sizes = (mesh.shape["lat"], mesh.shape["layer"], mesh.shape["freq"])
    return jax.shard_map(
        functools.partial(per_device, *sizes),
        mesh=mesh,
        in_specs=placed,
        out_specs=(P("layer", "lat", None), P("layer", None)),
        check_vma=False,
    )
```

time: 96.2 us -> 95.6 us (level)
  no operation moved by 1% of the time
where the time goes in v3:
time: 95.6 us; the launch traced here: 95.4 us
  Pallas kernels  92.8 us (97%)
  local copies, waits for them, and re-layouts  1.99 us (2%)
    pallas_call x1, Pallas kernels, per_device(): pl.pallas_call(functools.partial(kernel, lat, layers, freqs, n), out_shap...  92.8 us
    unnamed x4, local copies, waits for them, and re-layouts  1.99 us

profile of v3, /device:TPU:1, one launch (start us, length us, event | category | flops | bytes accessed | tf_op | source)
XLA Modules:
  0.0 95.4 jit_solution(3290254190788096509)
XLA Ops:
  0.6 92.8 %shard_map.86 = (f32[32,512]{1,0:T(8,128)}, f32[1,8]{1,0:T(1,128)}) custom-call(f32[2,2,32,512]{3,2,1,0:T(8,128)} %bitcast.7, f32[2,32,512]{2,1,0:T(8,128)} %bitcast.9, f32[16,32,512]{2,1,0:T(8,128)} %bitcast.6, f32[2,2,32,512]{3,2,1,0:T(8,128)} %bitcast.8, s32[32,512]{1,0:T(8,128)} %bitcast.10, bf16[3,512,256]{2,1,0:T(8,128)(2,1)} %constant.4.clone.high_hbm, ...), custom_call_target="tpu_custom_call" | custom-call | tf_op jit(solution)/shard_map/pallas_call | solution.py:455
  93.4 0.0 copy-start
  93.4 1.5 %copy.11 = f32[1,32,512]{2,1,0:T(8,128)} copy(f32[1,32,512]{2,1,0:T(8,128)} %bitcast.11) | data formatting | bytes 131072
  94.9 0.0 copy-done
  94.9 0.5 copy.12
Async XLA Ops:
  93.4 1.5 %copy-start = (f32[1,8]{1,0:T(1,128)S(1)}, f32[1,8]{1,0:T(1,128)}, u32[]{:S(2)}) copy-start(f32[1,8]{1,0:T(1,128)} %get-tuple-element.9) | copy-start | bytes 100

commit v4 on v3

--- a/solution.py
+++ b/solution.py
@@ -76,19 +76,31 @@
     sa_sem, ra_sem, sb_sem, rb_sem, sc_sem, rc_sem, sd_sem, rd_sem,
     sg_sem, rg_sem, st_sem, rt_sem, sl_sem, rl_sem, su_sem, ru_sem, sk_sem, rk_sem,
 ):
-    at = {"lat": lax.axis_index("lat"), "layer": lax.axis_index("layer"), "freq": lax.axis_index("freq")}
+    at = {axis: lax.axis_index(axis) for axis in ("lat", "layer", "freq")}
     size = {"lat": lat, "layer": layers, "freq": freqs}
+
+    def others(axis):
+        pair = 1 if axis == "freq" else 2
+        ring = size[axis] // pair
+        found = []
+        for k in range(size[axis] - 1):
+            i = k // pair
+            hop = ring // 2 - (i + 1) // 2 if i % 2 else ring - ring // 2 + i // 2
+            peer = lax.rem(at[axis] // pair + hop, ring) * pair
+            if pair == 2:
+                side = lax.rem(at[axis], 2)
+                peer = peer + (1 - side if k % 2 == 0 else side)
+            found.append((peer, {axis: peer}))
+        return found
+
+    peers = {axis: others(axis) for axis in at}
     half = n // 2
     wide = half // layers
 
     barrier = pltpu.get_barrier_semaphore()
     for axis in ("lat", "layer", "freq"):
-        def greet(k, carry, axis=axis):
-            peer = lax.rem(at[axis] + k, size[axis])
-            pl.semaphore_signal(barrier, inc=1, device_id={axis: peer}, device_id_type=MESH)
-            return carry
-        lax.fori_loop(1, size[axis], greet, 0)
-
+        for _, device in peers[axis]:
+            pl.semaphore_signal(barrier, inc=1, device_id=device, device_id_type=MESH)
     tiles = n // LANES
 
     def by_tile(i, source, target):
@@ -115,59 +127,45 @@
         for copy in loads[i]:
             copy.wait()
 
-    def remote(axis, peer, source, target, send_sem, recv_sem):
+    def remote(device, source, target, send_sem, recv_sem):
         return pltpu.make_async_remote_copy(
             src_ref=source, dst_ref=target, send_sem=send_sem, recv_sem=recv_sem,
-            device_id={axis: peer}, device_id_type=MESH,
+            device_id=device, device_id_type=MESH,
         )
 
-    def each_peer(axis, act):
-        pair = 1 if axis == "freq" else 2
-        ring = size[axis] // pair
-        def one(k, carry):
-            i = k // pair
-            ahead = i % 2
-            hop = ahead * (ring // 2 - (i + 1) // 2) + (1 - ahead) * (ring - ring // 2 + i // 2)
-            place = lax.rem(at[axis] // pair + hop, ring)
-            act(place * pair + (at[axis] + pair - 1 - k % pair) % pair)
-            return carry
-        lax.fori_loop(0, size[axis] - 1, one, 0)
+    def trade(axis, outgoing, landing, whole, mine, send_sem, recv_sem):
+        def everything():
+            return remote(peers[axis][0][1], whole[0], whole[1], send_sem, recv_sem)
+        def start():
+            for peer, device in peers[axis]:
+                remote(device, outgoing(peer), landing, send_sem, recv_sem).start()
+            if mine is not None:
+                mine().start()
+        def arrived():
+            if peers[axis]:
+                everything().wait_recv()
+            if mine is not None:
+                mine().wait()
+        def sent():
+            if peers[axis]:
+                everything().wait_send()
+        return start, arrived, sent
 
     def swap(axis, source, target, rows, send_sem, recv_sem, own):
-        me = at[axis]
         def block(ref, i):
             return ref.at[pl.ds(pl.multiple_of(i * rows, 8), rows)]
-        def copy(peer, landing):
-            return remote(axis, peer, block(source, peer), block(target, landing), send_sem.at[peer], recv_sem.at[landing])
         def mine():
-            return pltpu.make_async_copy(block(source, me), block(target, me), own)
-        def start():
-            each_peer(axis, lambda peer: copy(peer, me).start())
-            mine().start()
-        def arrived():
-            each_peer(axis, lambda peer: copy(peer, peer).wait_recv())
-            mine().wait()
-        def sent():
-            each_peer(axis, lambda peer: copy(peer, me).wait_send())
-        return start, arrived, sent
+            return pltpu.make_async_copy(block(source, at[axis]), block(target, at[axis]), own)
+        whole = tuple(ref.at[pl.ds(0, (size[axis] - 1) * rows)] for ref in (source, target))
+        return trade(axis, lambda peer: block(source, peer), block(target, at[axis]), whole, mine, send_sem, recv_sem)
 
     def spread(axis, source, target, send_sem, recv_sem, own):
-        me = at[axis]
-        def copy(peer, landing):
-            return remote(axis, peer, source, target.at[landing], send_sem.at[peer], recv_sem.at[landing])
         def mine():
-            return pltpu.make_async_copy(source, target.at[me], own)
-        def start():
-            each_peer(axis, lambda peer: copy(peer, me).start())
-            mine().start()
-        def arrived():
-            each_peer(axis, lambda peer: copy(peer, peer).wait_recv())
-            mine().wait()
-        def sent():
-            each_peer(axis, lambda peer: copy(peer, me).wait_send())
-        return start, arrived, sent
-
-    green_copies = swap("layer", send_g, recv_g, half, sg_sem, rg_sem, own_sem.at[16])
+            return pltpu.make_async_copy(source, target.at[at[axis]], own)
+        whole = (target.at[pl.ds(0, size[axis] - 1)],) * 2
+        return trade(axis, lambda peer: source, target.at[at[axis]], whole, mine, send_sem, recv_sem)
+
+    green_copies = swap("layer", send_g, recv_g, half, sg_sem.at[0], rg_sem.at[0], own_sem.at[16])
 
     def exchange(which, step, pol):
         axis, source, target, rows, send_sem, recv_sem = (
@@ -311,14 +309,15 @@
             if pol == 0:
                 @pl.when(step == 0)
                 def _():
+                    prepare_green()
                     pl.semaphore_wait(barrier, lat + layers + freqs - 3)
 
             exchange(0, step, pol)[0]()
 
-        @pl.when(step == 0)
-        def _():
-            prepare_green()
-            green_copies[0]()
+            if pol == 0:
+                @pl.when(step == 0)
+                def _():
+                    green_copies[0]()
 
         for pol in range(2):
             exchange(0, step, pol)[1]()
@@ -358,7 +357,7 @@
             spots = pl.ds(t * 32 + parity, 16, stride=2)
             terms[spots] = value if pol == 0 else terms[spots] + value
     own_rows = tiles * 32 // freqs
-    scatter = swap("freq", terms, recv_t, own_rows, st_sem, rt_sem, own_sem.at[17])
+    scatter = swap("freq", terms, recv_t, own_rows, st_sem.at[0], rt_sem.at[0], own_sem.at[17])
     scatter[0]()
 
     for c in range(CLASSES):
@@ -366,7 +365,7 @@
             jnp.where(cls[:, t * LANES:(t + 1) * LANES] == c, terms[t * 32:(t + 1) * 32], 0.0) for t in range(tiles)
         ]
         part[c:c + 1] = jnp.sum(sum(kept), axis=0, keepdims=True)
-    lat_sums = spread("lat", part, recv_l, sl_sem, rl_sem, own_sem.at[18])
+    lat_sums = spread("lat", part, recv_l, sl_sem.at[0], rl_sem.at[0], own_sem.at[18])
     lat_sums[0]()
 
     scatter[1]()
@@ -376,18 +375,16 @@
     own = pl.ds(pl.multiple_of(at["freq"] * own_rows, 8), own_rows)
     cell[own] = mine
 
-    def gather(peer, landing):
-        rows = pl.ds(pl.multiple_of(landing * own_rows, 8), own_rows)
-        return remote("freq", peer, cell.at[rows], cell.at[rows], su_sem.at[peer], ru_sem.at[landing])
-
-    each_peer("freq", lambda peer: gather(peer, at["freq"]).start())
+    spots = tuple(cell.at[pl.ds(0, (freqs - 1) * own_rows)] for _ in range(2))
+    gather = trade("freq", lambda peer: cell.at[own], cell.at[own], spots, None, su_sem.at[0], ru_sem.at[0])
+    gather[0]()
 
     lat_sums[1]()
     part_f[...] = jnp.sum(recv_l[...], axis=0)
-    freq_sums = spread("freq", part_f, recv_k, sk_sem, rk_sem, own_sem.at[19])
+    freq_sums = spread("freq", part_f, recv_k, sk_sem.at[0], rk_sem.at[0], own_sem.at[19])
     freq_sums[0]()
 
-    each_peer("freq", lambda peer: gather(peer, peer).wait_recv())
+    gather[1]()
     for t in range(tiles):
         cell_out[:, t * LANES:(t + 1) * LANES] = cell[t * 32:(t + 1) * 32]
     freq_sums[1]()
@@ -405,7 +402,7 @@
     green_copies[2]()
     scatter[2]()
     lat_sums[2]()
-    each_peer("freq", lambda peer: gather(peer, at["freq"]).wait_send())
+    gather[2]()
     freq_sums[2]()
 
 
@@ -444,13 +441,8 @@
         pltpu.VMEM((freqs, CLASSES, LANES), F32),
         dma((7, tiles)),
         dma((20,)),
-        *[dma((ITERS, 2, lat))] * 2,
-        *[dma((ITERS, 2, layers))] * 4,
-        *[dma((ITERS, 2, lat))] * 2,
-        *[dma((layers,))] * 2,
-        *[dma((freqs,))] * 2,
-        *[dma((lat,))] * 2,
-        *[dma((freqs,))] * 4,
+        *[dma((ITERS, 2))] * 8,
+        *[dma((1,))] * 10,
     ]
     cell, classes = pl.pallas_call(
         functools.partial(kernel, lat, layers, freqs, n),

time: 95.6 us -> 82.9 us (0.87)
  Pallas kernels: 92.8 us -> 79.7 us
    pallas_call x1, Pallas kernels: 92.8 us -> 79.7 us  [per_device(): pl.pallas_call(functools.partial(kernel, lat, layers, freqs, n), out_shap...]
where the time goes in v4:
time: 82.9 us; the launch traced here: 82.4 us
  Pallas kernels  79.7 us (96%)
  local copies, waits for them, and re-layouts  1.99 us (2%)
    pallas_call x1, Pallas kernels, per_device(): pl.pallas_call(functools.partial(kernel, lat, layers, freqs, n), out_shap...  79.7 us
    unnamed x4, local copies, waits for them, and re-layouts  1.99 us

profile of v4, /device:TPU:1, one launch (start us, length us, event | category | flops | bytes accessed | tf_op | source)
XLA Modules:
  0.0 82.4 jit_solution(13692369826378056106)
XLA Ops:
  0.6 79.7 %shard_map.86 = (f32[32,512]{1,0:T(8,128)}, f32[1,8]{1,0:T(1,128)}) custom-call(f32[2,2,32,512]{3,2,1,0:T(8,128)} %bitcast.7, f32[2,32,512]{2,1,0:T(8,128)} %bitcast.9, f32[16,32,512]{2,1,0:T(8,128)} %bitcast.6, f32[2,2,32,512]{3,2,1,0:T(8,128)} %bitcast.8, s32[32,512]{1,0:T(8,128)} %bitcast.10, bf16[3,512,256]{2,1,0:T(8,128)(2,1)} %constant.4.clone.high_hbm, ...), custom_call_target="tpu_custom_call" | custom-call | tf_op jit(solution)/shard_map/pallas_call | solution.py:447
  80.4 0.0 copy-start
  80.4 1.5 %copy.11 = f32[1,32,512]{2,1,0:T(8,128)} copy(f32[1,32,512]{2,1,0:T(8,128)} %bitcast.11) | data formatting | bytes 131072
  81.8 0.0 copy-done
  81.9 0.5 copy.12
Async XLA Ops:
  80.4 1.5 %copy-start = (f32[1,8]{1,0:T(1,128)S(1)}, f32[1,8]{1,0:T(1,128)}, u32[]{:S(2)}) copy-start(f32[1,8]{1,0:T(1,128)} %get-tuple-element.9) | copy-start | bytes 100

commit v5 on v4

--- a/solution.py
+++ b/solution.py
@@ -71,7 +71,7 @@
     src, con, field, rows_buf, cols_buf, prod,
     send_a, recv_a, send_b, recv_b, send_c, recv_c, send_d, recv_d,
     send_g, recv_g, wide_g,
-    terms, recv_t, cell, part, recv_l, part_f, recv_k,
+    terms, recv_t, cell, lines, part, recv_l, part_f, recv_k,
     load_sem, own_sem,
     sa_sem, ra_sem, sb_sem, rb_sem, sc_sem, rc_sem, sd_sem, rd_sem,
     sg_sem, rg_sem, st_sem, rt_sem, sl_sem, rl_sem, su_sem, ru_sem, sk_sem, rk_sem,
@@ -165,7 +165,11 @@
         whole = (target.at[pl.ds(0, size[axis] - 1)],) * 2
         return trade(axis, lambda peer: source, target.at[at[axis]], whole, mine, send_sem, recv_sem)
 
-    green_copies = swap("layer", send_g, recv_g, half, sg_sem.at[0], rg_sem.at[0], own_sem.at[16])
+    def green_block(ref, i):
+        return ref.at[pl.ds(pl.multiple_of(i * half, 8), half)]
+
+    def green_copy(device, peer, slot):
+        return remote(device, green_block(send_g, peer), green_block(recv_g, slot), sg_sem.at[0], rg_sem.at[slot])
 
     def exchange(which, step, pol):
         axis, source, target, rows, send_sem, recv_sem = (
@@ -257,12 +261,15 @@
                     row = ((tile * LANES // wide + part_of) * layers + pair) * wide
                     send_g[row:row + wide] = flipped[part_of * wide:(part_of + 1) * wide]
 
-    def widen(i, carry):
-        value = recv_g[pl.ds(pl.multiple_of(i * wide, 8), wide)]
-        odd = (lane_of(value.shape) // 32) % 2 == 1
-        wide_g[i * 2] = jnp.where(odd, pltpu.roll(value, 32, 1), value)
-        wide_g[i * 2 + 1] = jnp.where(odd, value, pltpu.roll(value, LANES - 32, 1))
-        return carry
+    def widen(source, l):
+        def one(pair, carry):
+            value = source[pl.ds(pl.multiple_of((l * layers + pair) * wide, 8), wide)]
+            odd = (lane_of(value.shape) // 32) % 2 == 1
+            spot = (l * layers + pair) * 2
+            wide_g[spot] = jnp.where(odd, pltpu.roll(value, 32, 1), value)
+            wide_g[spot + 1] = jnp.where(odd, value, pltpu.roll(value, LANES - 32, 1))
+            return carry
+        lax.fori_loop(0, layers, one, 0)
 
     def mix(step, pol):
         def rows(r, carry):
@@ -317,7 +324,8 @@
             if pol == 0:
                 @pl.when(step == 0)
                 def _():
-                    green_copies[0]()
+                    for peer, device in peers["layer"]:
+                        green_copy(device, peer, at["layer"]).start()
 
         for pol in range(2):
             exchange(0, step, pol)[1]()
@@ -327,8 +335,10 @@
 
         @pl.when(step == 0)
         def _():
-            green_copies[1]()
-            lax.fori_loop(0, layers * layers, widen, 0)
+            widen(send_g, at["layer"])
+            for peer, device in peers["layer"]:
+                green_copy(device, peer, peer).wait_recv()
+                widen(recv_g, peer)
 
         for pol in range(2):
             exchange(1, step, pol)[1]()
@@ -364,7 +374,10 @@
         kept = [
             jnp.where(cls[:, t * LANES:(t + 1) * LANES] == c, terms[t * 32:(t + 1) * 32], 0.0) for t in range(tiles)
         ]
-        part[c:c + 1] = jnp.sum(sum(kept), axis=0, keepdims=True)
+        lines[c:c + 1] = jnp.sum(sum(kept), axis=0, keepdims=True)
+    sums = jnp.sum(lines[...], axis=1, keepdims=True)
+    spot = lax.broadcasted_iota(jnp.int32, (CLASSES, LANES), 0) == lane_of((CLASSES, LANES))
+    part[...] = jnp.sum(jnp.where(spot, sums, 0.0), axis=0, keepdims=True)
     lat_sums = spread("lat", part, recv_l, sl_sem.at[0], rl_sem.at[0], own_sem.at[18])
     lat_sums[0]()
 
@@ -388,9 +401,7 @@
     for t in range(tiles):
         cell_out[:, t * LANES:(t + 1) * LANES] = cell[t * 32:(t + 1) * 32]
     freq_sums[1]()
-    sums = jnp.sum(jnp.sum(recv_k[...], axis=0), axis=1, keepdims=True) / float(n)
-    spot = lax.broadcasted_iota(jnp.int32, (CLASSES, LANES), 0) == lane_of((CLASSES, LANES))
-    class_out[...] = jnp.sum(jnp.where(spot, sums, 0.0), axis=0, keepdims=True)[:, :CLASSES]
+    class_out[...] = (jnp.sum(recv_k[...], axis=0) / float(n))[:, :CLASSES]
 
     def drain(step, carry):
         for pol in range(2):
@@ -399,7 +410,8 @@
         return carry
 
     lax.fori_loop(0, ITERS, drain, 0)
-    green_copies[2]()
+    for peer, device in peers["layer"]:
+        green_copy(device, peer, at["layer"]).wait_send()
     scatter[2]()
     lat_sums[2]()
     gather[2]()
@@ -436,13 +448,16 @@
         pltpu.VMEM((tiles * 32, LANES), F32),
         pltpu.VMEM((tiles * 32, LANES), F32),
         pltpu.VMEM((CLASSES, LANES), F32),
-        pltpu.VMEM((lat, CLASSES, LANES), F32),
-        pltpu.VMEM((CLASSES, LANES), F32),
-        pltpu.VMEM((freqs, CLASSES, LANES), F32),
+        pltpu.VMEM((1, LANES), F32),
+        pltpu.VMEM((lat, 1, LANES), F32),
+        pltpu.VMEM((1, LANES), F32),
+        pltpu.VMEM((freqs, 1, LANES), F32),
         dma((7, tiles)),
         dma((20,)),
         *[dma((ITERS, 2))] * 8,
-        *[dma((1,))] * 10,
+        dma((1,)),
+        dma((layers,)),
+        *[dma((1,))] * 8,
     ]
     cell, classes = pl.pallas_call(
         functools.partial(kernel, lat, layers, freqs, n),
@@ -451,7 +466,7 @@
         out_specs=(pl.BlockSpec(memory_space=pltpu.VMEM), pl.BlockSpec(memory_space=pltpu.VMEM)),
         scratch_shapes=scratch,
         compiler_params=pltpu.CompilerParams(
-            collective_id=0, has_side_effects=True
+            collective_id=0, has_side_effects=True, vmem_limit_bytes=55124 * 1024
         ),
     )(
         source.reshape(2, 2, 32, n),

time: 82.9 us -> 78.7 us (0.949)
  Pallas kernels: 79.7 us -> 76.5 us
  local copies, waits for them, and re-layouts: 1.99 us -> 1.14 us
    pallas_call x1, Pallas kernels: 79.7 us -> 76.5 us  [per_device(): pl.pallas_call(functools.partial(kernel, lat, layers, freqs, n), out_shap...]
    unnamed x4 -> x2, local copies, waits for them, and re-layouts: 1.99 us -> 1.14 us
where the time goes in v5:
time: 78.7 us; the launch traced here: 78.3 us
  Pallas kernels  76.5 us (97%)
  local copies, waits for them, and re-layouts  1.14 us (1%)
    pallas_call x1, Pallas kernels, per_device(): pl.pallas_call(functools.partial(kernel, lat, layers, freqs, n), out_shap...  76.5 us

profile of v5, /device:TPU:1, one launch (start us, length us, event | category | flops | bytes accessed | tf_op | source)
XLA Modules:
  0.0 78.3 jit_solution(14272976735180043626)
XLA Ops:
  0.6 76.5 %shard_map.86 = (f32[32,512]{1,0:T(8,128)S(1)}, f32[1,8]{1,0:T(1,128)S(1)}) custom-call(f32[2,2,32,512]{3,2,1,0:T(8,128)} %bitcast.8, f32[2,32,512]{2,1,0:T(8,128)} %bitcast.10, f32[16,32,512]{2,1,0:T(8,128)} %bitcast.7, f32[2,2,32,512]{3,2,1,0:T(8,128)} %bitcast.9, s32[32,512]{1,0:T(8,128)} %bitcast.11, bf16[3,512,256]{2,1,0:T(8,128)(2,1)} %constant.4.clone.high_hbm, ...), custom_call_target="tpu_custom_call" | custom-call | tf_op jit(solution)/shard_map/pallas_call | solution.py:462
  77.1 0.6 copy.11
  77.8 0.5 copy.12

commit v6 on v5

--- a/solution.py
+++ b/solution.py
@@ -198,11 +198,11 @@
         cols_buf[:, LANES:2 * LANES] = lower
         for i, table in enumerate((0, odd_table)):
             prod[i] = dot(high[table], cols_buf[...])
-        full = []
-        for i, table in enumerate((0, odd_table)):
-            tail = dot(low[table], cols_buf[:, 0:LANES])
-            full.append(prod[i, :, 0:LANES] + prod[i, :, LANES:2 * LANES] + tail)
-        both = jnp.where(lane_of(full[0].shape) < 64, full[0], full[1])
+        low_lanes = lane_of((n, LANES)) < 64
+        main = jnp.where(low_lanes, prod[0, :, 0:LANES], prod[1, :, 0:LANES])
+        main = main + jnp.where(low_lanes, prod[0, :, LANES:2 * LANES], prod[1, :, LANES:2 * LANES])
+        tails = [dot(low[table], cols_buf[:, 0:LANES]) for table in (0, odd_table)]
+        both = main + jnp.where(low_lanes, tails[0], tails[1])
         return both[:half], both[half:]
 
     def put_rows(parity, row, lanes, value):
@@ -262,14 +262,12 @@
                     send_g[row:row + wide] = flipped[part_of * wide:(part_of + 1) * wide]
 
     def widen(source, l):
-        def one(pair, carry):
+        for pair in range(layers):
             value = source[pl.ds(pl.multiple_of((l * layers + pair) * wide, 8), wide)]
             odd = (lane_of(value.shape) // 32) % 2 == 1
             spot = (l * layers + pair) * 2
             wide_g[spot] = jnp.where(odd, pltpu.roll(value, 32, 1), value)
             wide_g[spot + 1] = jnp.where(odd, value, pltpu.roll(value, LANES - 32, 1))
-            return carry
-        lax.fori_loop(0, layers, one, 0)
 
     def mix(step, pol):
         def rows(r, carry):
@@ -288,7 +286,7 @@
                 send_c[step, pol, pl.ds(pl.multiple_of(o * wide + base, 8), 8)] = sums[o]
             return carry
 
-        lax.fori_loop(0, wide // 8, rows, 0)
+        lax.fori_loop(0, wide // 8, rows, 0, unroll=2)
 
     even_odd = [(slice(parity * 16, parity * 16 + 16), pl.ds(parity, 16, stride=2)) for parity in range(2)]
     loaded(1)

time: 78.7 us -> 77.5 us (0.985)
  Pallas kernels: 76.5 us -> 75.3 us
    pallas_call x1, Pallas kernels: 76.5 us -> 75.3 us  [per_device(): pl.pallas_call(functools.partial(kernel, lat, layers, freqs, n), out_shap...]
where the time goes in v6:
time: 77.5 us; the launch traced here: 77.1 us
  Pallas kernels  75.3 us (97%)
  local copies, waits for them, and re-layouts  1.14 us (1%)
    pallas_call x1, Pallas kernels, per_device(): pl.pallas_call(functools.partial(kernel, lat, layers, freqs, n), out_shap...  75.3 us

profile of v6, /device:TPU:1, one launch (start us, length us, event | category | flops | bytes accessed | tf_op | source)
XLA Modules:
  0.0 77.1 jit_solution(5609692168571980532)
XLA Ops:
  0.6 75.3 %shard_map.86 = (f32[32,512]{1,0:T(8,128)S(1)}, f32[1,8]{1,0:T(1,128)S(1)}) custom-call(f32[2,2,32,512]{3,2,1,0:T(8,128)} %bitcast.8, f32[2,32,512]{2,1,0:T(8,128)} %bitcast.10, f32[16,32,512]{2,1,0:T(8,128)} %bitcast.7, f32[2,2,32,512]{3,2,1,0:T(8,128)} %bitcast.9, s32[32,512]{1,0:T(8,128)} %bitcast.11, bf16[3,512,256]{2,1,0:T(8,128)(2,1)} %constant.4.clone.high_hbm, ...), custom_call_target="tpu_custom_call" | custom-call | tf_op jit(solution)/shard_map/pallas_call | solution.py:460
  75.9 0.6 copy.11
  76.6 0.5 copy.12

commit v7 on v6

--- a/solution.py
+++ b/solution.py
@@ -82,14 +82,15 @@
     def others(axis):
         pair = 1 if axis == "freq" else 2
         ring = size[axis] // pair
+        spots = [(hop, flip) for hop in range(ring) for flip in range(pair) if hop or flip]
+        across = 1 if axis == "layer" else 0
+        spots.sort(key=lambda spot: (-min(spot[0], ring - spot[0]) - across * spot[1], -spot[1] * across, spot[1], spot[0]))
         found = []
-        for k in range(size[axis] - 1):
-            i = k // pair
-            hop = ring // 2 - (i + 1) // 2 if i % 2 else ring - ring // 2 + i // 2
+        for hop, flip in spots:
             peer = lax.rem(at[axis] // pair + hop, ring) * pair
             if pair == 2:
                 side = lax.rem(at[axis], 2)
-                peer = peer + (1 - side if k % 2 == 0 else side)
+                peer = peer + (1 - side if flip else side)
             found.append((peer, {axis: peer}))
         return found
 

time: 77.5 us -> 77.3 us (level)
  no operation moved by 1% of the time
where the time goes in v7:
time: 77.3 us; the launch traced here: 77.1 us
  Pallas kernels  75.4 us (98%)
  local copies, waits for them, and re-layouts  1.14 us (1%)
    pallas_call x1, Pallas kernels, per_device(): pl.pallas_call(functools.partial(kernel, lat, layers, freqs, n), out_shap...  75.4 us

profile of v7, /device:TPU:1, one launch (start us, length us, event | category | flops | bytes accessed | tf_op | source)
XLA Modules:
  0.0 77.1 jit_solution(15490824824533714560)
XLA Ops:
  0.6 75.4 %shard_map.86 = (f32[32,512]{1,0:T(8,128)S(1)}, f32[1,8]{1,0:T(1,128)S(1)}) custom-call(f32[2,2,32,512]{3,2,1,0:T(8,128)} %bitcast.8, f32[2,32,512]{2,1,0:T(8,128)} %bitcast.10, f32[16,32,512]{2,1,0:T(8,128)} %bitcast.7, f32[2,2,32,512]{3,2,1,0:T(8,128)} %bitcast.9, s32[32,512]{1,0:T(8,128)} %bitcast.11, bf16[3,512,256]{2,1,0:T(8,128)(2,1)} %constant.4.clone.high_hbm, ...), custom_call_target="tpu_custom_call" | custom-call | tf_op jit(solution)/shard_map/pallas_call | solution.py:461
  76.0 0.6 copy.11
  76.6 0.5 copy.12
